TPU v7x, 256 devices: a whole 4x4x8 slice. The times are simulated.
256 devices in a mesh: pipe: 8 (over x, y_hi), dp: 32 (over y_lo, z, core).
Axes of the slice: x: 4, y: 4 (y_hi: 2, y_lo: 2; y = y_hi * 2 + y_lo), z: 8, core: 2. Of those that a mesh axis runs over, the one named last changes fastest.
Arguments:
- tokens: bfloat16 [2, 64, 32, 4096], P(None, 'dp'), may hold values from -6 to 6
- cotangents: bfloat16 [2, 64, 32, 4096], P(None, 'dp'), may hold values from -1.5 to 1.5
- starts: int32 [2, 64, 4], P(None, 'dp'), may hold values from 0 to 31, as said below
- counts: int32 [2, 64], P(None, 'dp'), may hold values from 1 to 4
- layer_gains: bfloat16 [8, 4096], P('pipe', 'dp'), may hold values from 0.5 to 1.5
- first_map: bfloat16 [8, 4096, 128], P('pipe', 'dp'), may hold values from -0.09375 to 0.09375
- second_map: bfloat16 [8, 128, 4096], P('pipe', None, 'dp'), may hold values from -0.5 to 0.5
Outputs:
- gain_grad: float32 [8, 4096], P('pipe', 'dp')
- first_grad: float32 [8, 4096, 128], P('pipe', 'dp')
- second_grad: float32 [8, 128, 4096], P('pipe', None, 'dp')
Inputs may be any that keep to these rules, and one draw needn't show every extreme that they name: `starts`: each row begins with 0 and rises strictly; a micro-batch's documents begin at the first counts entries of its row, the later entries are not used.
All inputs are finite; a program needn't handle non-finite values.
Results may differ from a plain program's by a relative error of at most 0.03.
Values may be sent and summed in bfloat16 or wider, within the bound.
A program may use at most 64 MiB of HBM per device.

v0:
```python
import jax
import jax.numpy as jnp
from jax import lax
from jax.sharding import PartitionSpec as P

HD = 128


def partner(shard, axis, distance):
    return lax.ppermute(shard, axis, [(i, i ^ 1 << distance) for i in range(lax.axis_size(axis))])


def passed_along(value, axis, steps):
    count = lax.axis_size(axis)
    initial, last = (max(0, -steps), min(count, count - steps))
    return lax.ppermute(value, axis, [(source, source + steps) for source in range(initial, last)])


def shortened(shard):

    def short(part):
        return part.astype(jnp.bfloat16) if part.dtype == jnp.float32 else part

    return jax.tree.map(short, shard)


def doc_allowed(row_starts, row_count, length):
    positions = jnp.arange(length, dtype=jnp.int32)
    entries = jnp.arange(row_starts.shape[0], dtype=jnp.int32)
    started = (row_starts[None, :] <= positions[:, None]) & (entries < row_count)[None, :]
    document = jnp.sum(started.astype(jnp.int32), axis=1)
    matched = document[:, None] == document[None, :]
    return matched & (positions[None, :] <= positions[:, None])


def apply_layer(activation, gain_row, first_weight, second_weight, allowed):
    length = activation.shape[0]
    model_width = activation.shape[1]
    widened = activation.astype(jnp.float32)
    factor = lax.rsqrt(jnp.mean(widened * widened, axis=1, keepdims=True) + 1e-05)
    normed = (widened * factor * gain_row).astype(jnp.bfloat16)
    split_heads = normed.reshape(length, model_width // HD, HD)
    scores = (
        jnp.einsum("qhd,khd->hqk", split_heads, split_heads, preferred_element_type=jnp.float32)
        / HD
    )
    weights = jnp.where(allowed[None, :, :], jnp.exp(scores), 0.0)
    probabilities = (weights / jnp.sum(weights, axis=2, keepdims=True)).astype(jnp.bfloat16)
    mixed_heads = jnp.einsum(
        "hqk,khd->qhd", probabilities, split_heads, preferred_element_type=jnp.float32
    )
    mixed_heads = mixed_heads.reshape(length, model_width).astype(jnp.bfloat16)
    reduced = jnp.dot(mixed_heads, first_weight, preferred_element_type=jnp.float32).astype(
        jnp.bfloat16
    )
    return (widened + jnp.dot(reduced, second_weight, preferred_element_type=jnp.float32)).astype(
        jnp.bfloat16
    )


def layer_back(activation, gain_row, first_weight, second_weight, allowed, cotangent):
    _, pullback = jax.vjp(
        lambda act_in, gain_in, first_in, second_in: apply_layer(
            act_in, gain_in, first_in, second_in, allowed
        ),
        activation,
        gain_row,
        first_weight,
        second_weight,
    )
    return pullback(cotangent)


def add_masked(running_sums, gradients, live_flag):
    return tuple(
        (
            current + jnp.where(live_flag, gradient.astype(jnp.float32), 0.0)
            for current, gradient in zip(running_sums, gradients)
        )
    )


def round_parts(running_sums):
    return tuple(
        (lax.optimization_barrier(current.astype(jnp.bfloat16)) for current in running_sums)
    )


def per_device(tokens, cotangents, starts, counts, layer_gains, first_map, second_map):
    sections = lax.axis_size("pipe")
    my_section = lax.axis_index("pipe")
    bit_count = sections.bit_length() - 1
    micro_count = tokens.shape[1]
    length = tokens.shape[2]
    model_width = tokens.shape[3]
    tick_count = sections + micro_count - 1
    allowed_all = jax.vmap(
        jax.vmap(lambda row_starts, row_count: doc_allowed(row_starts, row_count, length))
    )(starts, counts)
    mirrored = (layer_gains, first_map, second_map)
    for bit_number in range(bit_count):
        mirrored = partner((mirrored[0], mirrored[1], mirrored[2]), "pipe", bit_number)
    stacked = (
        jnp.concatenate((layer_gains, mirrored[0]), axis=0),
        jnp.concatenate((first_map, mirrored[1]), axis=0),
        jnp.concatenate((second_map, mirrored[2]), axis=0),
    )
    full_gain, full_first, full_second = (
        lax.all_gather(stacked[0], "dp", axis=1, tiled=True),
        lax.all_gather(stacked[1], "dp", axis=1, tiled=True),
        lax.all_gather(stacked[2], "dp", axis=2, tiled=True),
    )

    def slot_of(index_value):
        live_flag = (index_value >= 0) & (index_value < micro_count)
        return (jnp.clip(index_value, 0, micro_count - 1), live_flag)

    def forward_tick(tick_index, loop_state):
        from_below, from_above, stashed = loop_state
        down_slot, down_live = slot_of(tick_index - my_section)
        up_slot, up_live = slot_of(tick_index - (sections - 1 - my_section))
        down_input = jnp.where(my_section == 0, tokens[0, down_slot], from_below)
        up_input = jnp.where(my_section == sections - 1, tokens[1, up_slot], from_above)
        down_output = apply_layer(
            down_input, full_gain[0], full_first[0], full_second[0], allowed_all[0, down_slot]
        )
        up_output = apply_layer(
            up_input, full_gain[1], full_first[1], full_second[1], allowed_all[1, up_slot]
        )
        stashed = stashed.at[0, down_slot].set(
            jnp.where(down_live, down_input, stashed[0, down_slot])
        )
        stashed = stashed.at[1, up_slot].set(jnp.where(up_live, up_input, stashed[1, up_slot]))
        from_below = passed_along(down_output, "pipe", 1)
        from_above = passed_along(up_output, "pipe", -1)
        return (from_below, from_above, stashed)

    empty_rows = jnp.zeros((length, model_width), jnp.bfloat16)
    empty_stash = jnp.zeros((2, micro_count, length, model_width), jnp.bfloat16)
    _, _, stashed = lax.fori_loop(
        0, tick_count, forward_tick, (empty_rows, empty_rows, empty_stash)
    )
    zero_sums = (
        jnp.zeros((model_width,), jnp.float32),
        jnp.zeros((model_width, first_map.shape[2]), jnp.float32),
        jnp.zeros((second_map.shape[1], model_width), jnp.float32),
    )

    def backward_tick(tick_index, loop_state):
        from_above, from_below, down_sums, up_sums = loop_state
        down_slot, down_live = slot_of(tick_index - (sections - 1 - my_section))
        up_slot, up_live = slot_of(tick_index - my_section)
        down_cot = jnp.where(my_section == sections - 1, cotangents[0, down_slot], from_above)
        up_cot = jnp.where(my_section == 0, cotangents[1, up_slot], from_below)
        down_back = layer_back(
            stashed[0, down_slot],
            full_gain[0],
            full_first[0],
            full_second[0],
            allowed_all[0, down_slot],
            down_cot,
        )
        up_back = layer_back(
            stashed[1, up_slot],
            full_gain[1],
            full_first[1],
            full_second[1],
            allowed_all[1, up_slot],
            up_cot,
        )
        down_sums = add_masked(down_sums, down_back[1:], down_live)
        up_sums = add_masked(up_sums, up_back[1:], up_live)
        from_above = passed_along(down_back[0], "pipe", -1)
        from_below = passed_along(up_back[0], "pipe", 1)
        return (from_above, from_below, down_sums, up_sums)

    _, _, down_sums, up_sums = lax.fori_loop(
        0, tick_count, backward_tick, (empty_rows, empty_rows, zero_sums, zero_sums)
    )
    down_parts = round_parts(down_sums)
    up_parts = round_parts(up_sums)
    received = up_parts
    for bit_number in range(bit_count):
        received = jax.tree.map(
            lambda part, own: part.astype(own.dtype),
            partner(shortened(received), "pipe", bit_number),
            received,
        )
    pair_sums = tuple(
        (
            own_part.astype(jnp.float32) + other_part.astype(jnp.float32)
            for own_part, other_part in zip(down_parts, received)
        )
    )
    gain_total, first_total, second_total = (
        lax.psum_scatter(
            pair_sums[0].astype(jnp.bfloat16), "dp", scatter_dimension=0, tiled=True
        ).astype(jnp.float32),
        lax.psum_scatter(
            pair_sums[1].astype(jnp.bfloat16), "dp", scatter_dimension=0, tiled=True
        ).astype(jnp.float32),
        lax.psum_scatter(
            pair_sums[2].astype(jnp.bfloat16), "dp", scatter_dimension=1, tiled=True
        ).astype(jnp.float32),
    )
    return (gain_total[None], first_total[None], second_total[None])


def solution(mesh):
    in_specs = (
        P(None, "dp", None, None),
        P(None, "dp", None, None),
        P(None, "dp", None),
        P(None, "dp"),
        P("pipe", "dp"),
        P("pipe", "dp", None),
        P("pipe", None, "dp"),
    )
    out_specs = (P("pipe", "dp"), P("pipe", "dp", None), P("pipe", None, "dp"))
    return jax.shard_map(
        per_device, mesh=mesh, in_specs=in_specs, out_specs=out_specs, check_vma=False
    )
```

profile of v0, /device:TPU:2, one launch (start us, length us, event | category | flops | bytes accessed | tf_op | source)
XLA Modules:
  0.0 1092.7 jit_solution(12410242168434772746)
XLA Ops:
  55.1 37.2 %all_gather.11 = bf16[2,4096]{1,0:T(2,128)(2,1)S(1)} all-gather(bf16[2,128]{1,0:T(2,128)(2,1)S(1)} %pad_maximum_fusion.2), channel_id=1, replica_groups=mesh['pipe'=8,'dp'=32] {'dp'}, dimensions={1}, use_global_device_ids=true | all-gather | bytes 16896 | tf_op jit(solution)/shard_map/all_gather | solution.py:109
  92.3 65.1 %all-gather.5.cloned.1.call-done = bf16[2,4096,128]{2,1,0:T(8,128)(2,1)} async-done(((bf16[2,128,128]{2,1,0:T(8,128)(2,1)}), bf16[2,4096,128]{2,1,0:T(8,128)(2,1)}) %all-gather.5.cloned.1.call-update) | async-done | bytes 2097168 | tf_op jit(solution)/shard_map/all_gather | solution.py:110
  158.2 282.0 %while.49 = (s32[]{:T(128)}, bf16[32,4096]{1,0:T(8,128)(2,1)S(1)}, bf16[32,4096]{1,0:T(8,128)(2,1)}, bf16[2,2,32,4096]{3,2,1,0:T(8,128)(2,1)S(1)}, pred[]{:T(512...) while((s32[]{:T(128)}, bf16[32,4096]{1,0:T(8,128)(2,1)S(1)}, ...), condition=%wide.region_8.9_spmd, body=%wide.region_1.8_spmd.sunk | while | flops 172771520 | bytes 23715560 | solution.py:140
  170.0 4.6 collective-permute-start.1
  183.5 9.9 collective-permute-done
  213.3 5.4 collective-permute-start
  218.7 6.4 collective-permute-done
  244.9 5.4 collective-permute-start
  250.4 5.5 collective-permute-done
  275.7 5.4 collective-permute-start
  281.2 5.4 collective-permute-done
  306.4 5.4 collective-permute-start
  311.9 5.4 collective-permute-done
  337.2 5.4 collective-permute-start
  342.6 5.4 collective-permute-done
  367.9 5.4 collective-permute-start
  373.3 5.4 collective-permute-done
  398.6 5.4 collective-permute-start
  404.1 5.4 collective-permute-done
  429.4 5.4 collective-permute-start
  434.8 5.4 collective-permute-done
  441.7 323.3 %while.50 = (s32[]{:T(128)}, bf16[32,4096]{1,0:T(8,128)(2,1)}, bf16[32,4096]{1,0:T(8,128)(2,1)}, f32[4096]{0:T(1024)S(1)}, f32[4096,128]{1,0:T(8,128)}, /*index=...) while((s32[]{:T(128)}, bf16[32,4096]{1,0:T(8,128)(2,1)}, ...), condition=%wide.region_20.21_spmd.clone, body=%wide.region_9.20_spmd.clone.sunk | while | flops 456771968 | bytes 73035120 | solution.py:177
  454.0 5.4 collective-permute-start.3
  487.5 4.5 collective-permute-start.3
  495.2 3.9 fusion.335
  502.5 3.7 fusion.338
  523.9 4.5 collective-permute-start.3
  531.6 3.9 fusion.335
  538.9 3.7 fusion.338
  556.7 3.7 collective-permute-start.2
  560.4 4.5 collective-permute-start.3
  568.0 3.9 fusion.335
  575.4 3.7 fusion.338
  593.1 3.7 collective-permute-start.2
  596.8 4.5 collective-permute-start.3
  604.5 3.9 fusion.335
  611.8 3.7 fusion.338
  629.6 3.7 collective-permute-start.2
  633.3 4.5 collective-permute-start.3
  640.9 3.9 fusion.335
  648.3 3.7 fusion.338
  666.0 3.7 collective-permute-start.2
  669.7 4.5 collective-permute-start.3
  677.4 3.9 fusion.335
  684.7 3.7 fusion.338
  706.2 4.5 collective-permute-start.3
  713.8 3.9 fusion.335
  721.2 3.7 fusion.338
  738.9 3.7 collective-permute-start.2
  742.6 4.5 collective-permute-start.3
  750.3 3.9 fusion.335
  757.6 3.7 fusion.338
  766.8 4.5 collective-permute-start.19
  771.3 19.6 %collective-permute-done.19 = bf16[128,4096]{1,0:T(8,128)(2,1)S(1)} collective-permute-done((bf16[128,4096]{1,0:T(8,128)(2,1)S(1)}, bf16[128,4096]{1,0:T(8,128)(2,1)S(1)}, u32[]{:S(2)}, u32[]{:S(2)}) %collective-permute-start.19) | collective-permute-done | bytes 1048608 | tf_op jit(solution)/shard_map/ppermute | solution.py:10
  791.0 4.0 collective-permute-start.16
  795.1 21.9 %collective-permute-done.20 = bf16[128,4096]{1,0:T(8,128)(2,1)S(1)} collective-permute-done((bf16[128,4096]{1,0:T(8,128)(2,1)S(1)}, bf16[128,4096]{1,0:T(8,128)(2,1)S(1)}, u32[]{:S(2)}, u32[]{:S(2)}) %collective-permute-start.20) | collective-permute-done | bytes 1048608 | tf_op jit(solution)/shard_map/ppermute | solution.py:10
  816.9 7.6 collective-permute-start.21
  825.4 19.1 %collective-permute-done.21 = bf16[128,4096]{1,0:T(8,128)(2,1)S(1)} collective-permute-done((bf16[128,4096]{1,0:T(8,128)(2,1)S(1)}, bf16[128,4096]{1,0:T(8,128)(2,1)S(1)}, u32[]{:S(2)}, u32[]{:S(2)}) %collective-permute-start.21) | collective-permute-done | bytes 1048608 | tf_op jit(solution)/shard_map/ppermute | solution.py:10
  848.3 13.1 %collective-permute-done.17 = bf16[4096,128]{1,0:T(8,128)(2,1)} collective-permute-done((bf16[4096,128]{1,0:T(8,128)(2,1)}, bf16[4096,128]{1,0:T(8,128)(2,1)}, u32[]{:S(2)}, u32[]{:S(2)}) %collective-permute-start.17) | collective-permute-done | bytes 1048608 | tf_op jit(solution)/shard_map/ppermute | solution.py:10
  861.5 16.5 %collective-permute-done.18 = bf16[4096,128]{1,0:T(8,128)(2,1)S(1)} collective-permute-done((bf16[4096,128]{1,0:T(8,128)(2,1)}, bf16[4096,128]{1,0:T(8,128)(2,1)S(1)}, u32[]{:S(2)}, u32[]{:S(2)}) %collective-permute-start.18) | collective-permute-done | bytes 1048608 | tf_op jit(solution)/shard_map/ppermute | solution.py:10
  889.5 3.9 collective-permute-done.15
  893.4 54.2 %all-reduce = bf16[4096]{0:T(1024)(128)(2,1)S(1)} all-reduce(bf16[4096]{0:T(1024)(128)(2,1)S(1)} %add_convert_fusion.2), channel_id=2, replica_groups=mesh['pipe'=8,'dp'=32] {'dp'}, use_global_device_ids=true, to_apply=%region_21.22.clone | all-reduce | flops 4096 | bytes 16384
  948.2 20.0 %reduce-scatter.7.cloned.1.call-done = bf16[128,128]{1,0:T(8,128)(2,1)} async-done(((bf16[4096,128]{1,0:T(8,128)(2,1)}), bf16[128,128]{1,0:T(8,128)(2,1)}) %reduce-scatter.7.cloned.1.call-update) | async-done | bytes 32784
  969.7 115.0 %reduce-scatter.5.cloned.1.call-done = bf16[128,128]{1,0:T(8,128)(2,1)} async-done(((bf16[4096,128]{1,0:T(8,128)(2,1)}), bf16[128,128]{1,0:T(8,128)(2,1)}) %reduce-scatter.5.cloned.1.call-update) | async-done | bytes 32784 | tf_op jit(solution)/shard_map/reduce_scatter | solution.py:199
  (767 shorter events, 449.4 us)
Async XLA Ops:
  7.2 85.1 %all-gather.3.cloned.1.call-start = ((), (), s32[]{:S(2)}) async-start(), calls=%async_computation.2 | async-start | bytes 2162688 | tf_op jit(solution)/shard_map/all_gather | solution.py:111
  7.2 5.7 collective-permute-start.4
  12.9 4.1 collective-permute-start.5
  17.1 5.4 collective-permute-start.6
  23.9 133.4 %all-gather.5.cloned.1.call-start = ((), (), s32[]{:S(2)}) async-start(), calls=%async_computation.3 | async-start | bytes 2162688 | tf_op jit(solution)/shard_map/all_gather | solution.py:110
  23.9 5.7 collective-permute-start.7
  29.7 3.9 collective-permute-start.8
  33.6 5.4 collective-permute-start.9
  40.4 927.8 %reduce-scatter.7.cloned.1.call-start = ((), (), s32[]{:S(2)}) async-start(), calls=%async_computation.5 | async-start | bytes 1081344
  40.5 5.3 collective-permute-start.10
  45.8 3.6 collective-permute-start.11
  49.3 5.1 collective-permute-start.12
  170.0 13.5 %collective-permute-start.1 = (bf16[32,4096]{1,0:T(8,128)(2,1)}, bf16[32,4096]{1,0:T(8,128)(2,1)}, u32[]{:S(2)}, u32[]{:S(2)}) collective-permute-start(bf16[32,4096]{1,0:T(8,128)(2,1)} %fusion.286), channel_id=1, source_target_pairs={{32,0},{64,32},{96,64},{128,96},{160,128},{192,160},{224,192},{33,... | collective-permute-start | bytes 786440 | tf_op jit(solution)/shard_map/while/body/eval_jaxpr/ppermute | solution.py:16
  180.8 12.6 %collective-permute-start = (bf16[32,4096]{1,0:T(8,128)(2,1)}, bf16[32,4096]{1,0:T(8,128)(2,1)S(1)}, u32[]{:S(2)}, u32[]{:S(2)}) collective-permute-start(bf16[32,4096]{1,0:T(8,128)(2,1)} %fusion.281), channel_id=1, source_target_pairs={{0,32},{32,64},{64,96},{96,128},{128,160},{160,192},{192,224},{1,3... | collective-permute-start | bytes 786440 | tf_op jit(solution)/shard_map/while/body/eval_jaxpr/ppermute | solution.py:16
  205.2 13.5 %collective-permute-start.1 = (bf16[32,4096]{1,0:T(8,128)(2,1)}, bf16[32,4096]{1,0:T(8,128)(2,1)}, u32[]{:S(2)}, u32[]{:S(2)}) collective-permute-start(bf16[32,4096]{1,0:T(8,128)(2,1)} %fusion.286), channel_id=1, source_target_pairs={{32,0},{64,32},{96,64},{128,96},{160,128},{192,160},{224,192},{33,... | collective-permute-start | bytes 786440 | tf_op jit(solution)/shard_map/while/body/eval_jaxpr/ppermute | solution.py:16
  213.3 11.8 %collective-permute-start = (bf16[32,4096]{1,0:T(8,128)(2,1)}, bf16[32,4096]{1,0:T(8,128)(2,1)S(1)}, u32[]{:S(2)}, u32[]{:S(2)}) collective-permute-start(bf16[32,4096]{1,0:T(8,128)(2,1)} %fusion.281), channel_id=1, source_target_pairs={{0,32},{32,64},{64,96},{96,128},{128,160},{160,192},{192,224},{1,3... | collective-permute-start | bytes 786440 | tf_op jit(solution)/shard_map/while/body/eval_jaxpr/ppermute | solution.py:16
  236.9 13.5 %collective-permute-start.1 = (bf16[32,4096]{1,0:T(8,128)(2,1)}, bf16[32,4096]{1,0:T(8,128)(2,1)}, u32[]{:S(2)}, u32[]{:S(2)}) collective-permute-start(bf16[32,4096]{1,0:T(8,128)(2,1)} %fusion.286), channel_id=1, source_target_pairs={{32,0},{64,32},{96,64},{128,96},{160,128},{192,160},{224,192},{33,... | collective-permute-start | bytes 786440 | tf_op jit(solution)/shard_map/while/body/eval_jaxpr/ppermute | solution.py:16
  244.9 10.9 %collective-permute-start = (bf16[32,4096]{1,0:T(8,128)(2,1)}, bf16[32,4096]{1,0:T(8,128)(2,1)S(1)}, u32[]{:S(2)}, u32[]{:S(2)}) collective-permute-start(bf16[32,4096]{1,0:T(8,128)(2,1)} %fusion.281), channel_id=1, source_target_pairs={{0,32},{32,64},{64,96},{96,128},{128,160},{160,192},{192,224},{1,3... | collective-permute-start | bytes 786440 | tf_op jit(solution)/shard_map/while/body/eval_jaxpr/ppermute | solution.py:16
  267.7 13.5 %collective-permute-start.1 = (bf16[32,4096]{1,0:T(8,128)(2,1)}, bf16[32,4096]{1,0:T(8,128)(2,1)}, u32[]{:S(2)}, u32[]{:S(2)}) collective-permute-start(bf16[32,4096]{1,0:T(8,128)(2,1)} %fusion.286), channel_id=1, source_target_pairs={{32,0},{64,32},{96,64},{128,96},{160,128},{192,160},{224,192},{33,... | collective-permute-start | bytes 786440 | tf_op jit(solution)/shard_map/while/body/eval_jaxpr/ppermute | solution.py:16
  275.7 10.9 collective-permute-start
  298.4 13.5 %collective-permute-start.1 = (bf16[32,4096]{1,0:T(8,128)(2,1)}, bf16[32,4096]{1,0:T(8,128)(2,1)}, u32[]{:S(2)}, u32[]{:S(2)}) collective-permute-start(bf16[32,4096]{1,0:T(8,128)(2,1)} %fusion.286), channel_id=1, source_target_pairs={{32,0},{64,32},{96,64},{128,96},{160,128},{192,160},{224,192},{33,... | collective-permute-start | bytes 786440 | tf_op jit(solution)/shard_map/while/body/eval_jaxpr/ppermute | solution.py:16
  306.4 10.9 collective-permute-start
  329.1 13.5 %collective-permute-start.1 = (bf16[32,4096]{1,0:T(8,128)(2,1)}, bf16[32,4096]{1,0:T(8,128)(2,1)}, u32[]{:S(2)}, u32[]{:S(2)}) collective-permute-start(bf16[32,4096]{1,0:T(8,128)(2,1)} %fusion.286), channel_id=1, source_target_pairs={{32,0},{64,32},{96,64},{128,96},{160,128},{192,160},{224,192},{33,... | collective-permute-start | bytes 786440 | tf_op jit(solution)/shard_map/while/body/eval_jaxpr/ppermute | solution.py:16
  337.2 10.9 collective-permute-start
  359.9 13.5 %collective-permute-start.1 = (bf16[32,4096]{1,0:T(8,128)(2,1)}, bf16[32,4096]{1,0:T(8,128)(2,1)}, u32[]{:S(2)}, u32[]{:S(2)}) collective-permute-start(bf16[32,4096]{1,0:T(8,128)(2,1)} %fusion.286), channel_id=1, source_target_pairs={{32,0},{64,32},{96,64},{128,96},{160,128},{192,160},{224,192},{33,... | collective-permute-start | bytes 786440 | tf_op jit(solution)/shard_map/while/body/eval_jaxpr/ppermute | solution.py:16
  367.9 10.9 collective-permute-start
  390.6 13.5 %collective-permute-start.1 = (bf16[32,4096]{1,0:T(8,128)(2,1)}, bf16[32,4096]{1,0:T(8,128)(2,1)}, u32[]{:S(2)}, u32[]{:S(2)}) collective-permute-start(bf16[32,4096]{1,0:T(8,128)(2,1)} %fusion.286), channel_id=1, source_target_pairs={{32,0},{64,32},{96,64},{128,96},{160,128},{192,160},{224,192},{33,... | collective-permute-start | bytes 786440 | tf_op jit(solution)/shard_map/while/body/eval_jaxpr/ppermute | solution.py:16
  398.6 10.9 collective-permute-start
  421.3 13.5 %collective-permute-start.1 = (bf16[32,4096]{1,0:T(8,128)(2,1)}, bf16[32,4096]{1,0:T(8,128)(2,1)}, u32[]{:S(2)}, u32[]{:S(2)}) collective-permute-start(bf16[32,4096]{1,0:T(8,128)(2,1)} %fusion.286), channel_id=1, source_target_pairs={{32,0},{64,32},{96,64},{128,96},{160,128},{192,160},{224,192},{33,... | collective-permute-start | bytes 786440 | tf_op jit(solution)/shard_map/while/body/eval_jaxpr/ppermute | solution.py:16
  429.4 10.9 collective-permute-start
  444.8 6.4 copy-start.3
  452.1 22.1 %collective-permute-start.2 = (bf16[32,4096]{1,0:T(8,128)(2,1)}, bf16[32,4096]{1,0:T(8,128)(2,1)}, u32[]{:S(2)}, u32[]{:S(2)}) collective-permute-start(bf16[32,4096]{1,0:T(8,128)(2,1)} %fusion.332), channel_id=1, source_target_pairs={{32,0},{64,32},{96,64},{128,96},{160,128},{192,160},{224,192},{33,... | collective-permute-start | bytes 786440 | tf_op jit(solution)/shard_map/while/body/eval_jaxpr/ppermute | solution.py:16
  454.0 20.2 %collective-permute-start.3 = (bf16[32,4096]{1,0:T(8,128)(2,1)}, bf16[32,4096]{1,0:T(8,128)(2,1)}, u32[]{:S(2)}, u32[]{:S(2)}) collective-permute-start(bf16[32,4096]{1,0:T(8,128)(2,1)} %get-tuple-element.1028), channel_id=1, source_target_pairs={{0,32},{32,64},{64,96},{96,128},{128,160},{160,192},{192,224},{1,3... | collective-permute-start | bytes 786440 | tf_op jit(solution)/shard_map/while/body/eval_jaxpr/ppermute | solution.py:16
  477.4 6.4 copy-start.3
  484.7 25.1 %collective-permute-start.2 = (bf16[32,4096]{1,0:T(8,128)(2,1)}, bf16[32,4096]{1,0:T(8,128)(2,1)}, u32[]{:S(2)}, u32[]{:S(2)}) collective-permute-start(bf16[32,4096]{1,0:T(8,128)(2,1)} %fusion.332), channel_id=1, source_target_pairs={{32,0},{64,32},{96,64},{128,96},{160,128},{192,160},{224,192},{33,... | collective-permute-start | bytes 786440 | tf_op jit(solution)/shard_map/while/body/eval_jaxpr/ppermute | solution.py:16
  487.5 22.3 %collective-permute-start.3 = (bf16[32,4096]{1,0:T(8,128)(2,1)}, bf16[32,4096]{1,0:T(8,128)(2,1)}, u32[]{:S(2)}, u32[]{:S(2)}) collective-permute-start(bf16[32,4096]{1,0:T(8,128)(2,1)} %get-tuple-element.1028), channel_id=1, source_target_pairs={{0,32},{32,64},{64,96},{96,128},{128,160},{160,192},{192,224},{1,3... | collective-permute-start | bytes 786440 | tf_op jit(solution)/shard_map/while/body/eval_jaxpr/ppermute | solution.py:16
  520.2 26.0 %collective-permute-start.2 = (bf16[32,4096]{1,0:T(8,128)(2,1)}, bf16[32,4096]{1,0:T(8,128)(2,1)}, u32[]{:S(2)}, u32[]{:S(2)}) collective-permute-start(bf16[32,4096]{1,0:T(8,128)(2,1)} %fusion.332), channel_id=1, source_target_pairs={{32,0},{64,32},{96,64},{128,96},{160,128},{192,160},{224,192},{33,... | collective-permute-start | bytes 786440 | tf_op jit(solution)/shard_map/while/body/eval_jaxpr/ppermute | solution.py:16
  523.9 22.3 %collective-permute-start.3 = (bf16[32,4096]{1,0:T(8,128)(2,1)}, bf16[32,4096]{1,0:T(8,128)(2,1)}, u32[]{:S(2)}, u32[]{:S(2)}) collective-permute-start(bf16[32,4096]{1,0:T(8,128)(2,1)} %get-tuple-element.1028), channel_id=1, source_target_pairs={{0,32},{32,64},{64,96},{96,128},{128,160},{160,192},{192,224},{1,3... | collective-permute-start | bytes 786440 | tf_op jit(solution)/shard_map/while/body/eval_jaxpr/ppermute | solution.py:16
  556.7 26.0 %collective-permute-start.2 = (bf16[32,4096]{1,0:T(8,128)(2,1)}, bf16[32,4096]{1,0:T(8,128)(2,1)}, u32[]{:S(2)}, u32[]{:S(2)}) collective-permute-start(bf16[32,4096]{1,0:T(8,128)(2,1)} %fusion.332), channel_id=1, source_target_pairs={{32,0},{64,32},{96,64},{128,96},{160,128},{192,160},{224,192},{33,... | collective-permute-start | bytes 786440 | tf_op jit(solution)/shard_map/while/body/eval_jaxpr/ppermute | solution.py:16
  560.4 22.3 %collective-permute-start.3 = (bf16[32,4096]{1,0:T(8,128)(2,1)}, bf16[32,4096]{1,0:T(8,128)(2,1)}, u32[]{:S(2)}, u32[]{:S(2)}) collective-permute-start(bf16[32,4096]{1,0:T(8,128)(2,1)} %get-tuple-element.1028), channel_id=1, source_target_pairs={{0,32},{32,64},{64,96},{96,128},{128,160},{160,192},{192,224},{1,3... | collective-permute-start | bytes 786440 | tf_op jit(solution)/shard_map/while/body/eval_jaxpr/ppermute | solution.py:16
  593.1 26.0 %collective-permute-start.2 = (bf16[32,4096]{1,0:T(8,128)(2,1)}, bf16[32,4096]{1,0:T(8,128)(2,1)}, u32[]{:S(2)}, u32[]{:S(2)}) collective-permute-start(bf16[32,4096]{1,0:T(8,128)(2,1)} %fusion.332), channel_id=1, source_target_pairs={{32,0},{64,32},{96,64},{128,96},{160,128},{192,160},{224,192},{33,... | collective-permute-start | bytes 786440 | tf_op jit(solution)/shard_map/while/body/eval_jaxpr/ppermute | solution.py:16
  596.8 22.3 %collective-permute-start.3 = (bf16[32,4096]{1,0:T(8,128)(2,1)}, bf16[32,4096]{1,0:T(8,128)(2,1)}, u32[]{:S(2)}, u32[]{:S(2)}) collective-permute-start(bf16[32,4096]{1,0:T(8,128)(2,1)} %get-tuple-element.1028), channel_id=1, source_target_pairs={{0,32},{32,64},{64,96},{96,128},{128,160},{160,192},{192,224},{1,3... | collective-permute-start | bytes 786440 | tf_op jit(solution)/shard_map/while/body/eval_jaxpr/ppermute | solution.py:16
  629.6 26.0 %collective-permute-start.2 = (bf16[32,4096]{1,0:T(8,128)(2,1)}, bf16[32,4096]{1,0:T(8,128)(2,1)}, u32[]{:S(2)}, u32[]{:S(2)}) collective-permute-start(bf16[32,4096]{1,0:T(8,128)(2,1)} %fusion.332), channel_id=1, source_target_pairs={{32,0},{64,32},{96,64},{128,96},{160,128},{192,160},{224,192},{33,... | collective-permute-start | bytes 786440 | tf_op jit(solution)/shard_map/while/body/eval_jaxpr/ppermute | solution.py:16
  633.3 22.3 %collective-permute-start.3 = (bf16[32,4096]{1,0:T(8,128)(2,1)}, bf16[32,4096]{1,0:T(8,128)(2,1)}, u32[]{:S(2)}, u32[]{:S(2)}) collective-permute-start(bf16[32,4096]{1,0:T(8,128)(2,1)} %get-tuple-element.1028), channel_id=1, source_target_pairs={{0,32},{32,64},{64,96},{96,128},{128,160},{160,192},{192,224},{1,3... | collective-permute-start | bytes 786440 | tf_op jit(solution)/shard_map/while/body/eval_jaxpr/ppermute | solution.py:16
  666.0 26.0 %collective-permute-start.2 = (bf16[32,4096]{1,0:T(8,128)(2,1)}, bf16[32,4096]{1,0:T(8,128)(2,1)}, u32[]{:S(2)}, u32[]{:S(2)}) collective-permute-start(bf16[32,4096]{1,0:T(8,128)(2,1)} %fusion.332), channel_id=1, source_target_pairs={{32,0},{64,32},{96,64},{128,96},{160,128},{192,160},{224,192},{33,... | collective-permute-start | bytes 786440 | tf_op jit(solution)/shard_map/while/body/eval_jaxpr/ppermute | solution.py:16
  669.7 22.3 %collective-permute-start.3 = (bf16[32,4096]{1,0:T(8,128)(2,1)}, bf16[32,4096]{1,0:T(8,128)(2,1)}, u32[]{:S(2)}, u32[]{:S(2)}) collective-permute-start(bf16[32,4096]{1,0:T(8,128)(2,1)} %get-tuple-element.1028), channel_id=1, source_target_pairs={{0,32},{32,64},{64,96},{96,128},{128,160},{160,192},{192,224},{1,3... | collective-permute-start | bytes 786440 | tf_op jit(solution)/shard_map/while/body/eval_jaxpr/ppermute | solution.py:16
  702.5 26.0 %collective-permute-start.2 = (bf16[32,4096]{1,0:T(8,128)(2,1)}, bf16[32,4096]{1,0:T(8,128)(2,1)}, u32[]{:S(2)}, u32[]{:S(2)}) collective-permute-start(bf16[32,4096]{1,0:T(8,128)(2,1)} %fusion.332), channel_id=1, source_target_pairs={{32,0},{64,32},{96,64},{128,96},{160,128},{192,160},{224,192},{33,... | collective-permute-start | bytes 786440 | tf_op jit(solution)/shard_map/while/body/eval_jaxpr/ppermute | solution.py:16
  706.2 22.3 %collective-permute-start.3 = (bf16[32,4096]{1,0:T(8,128)(2,1)}, bf16[32,4096]{1,0:T(8,128)(2,1)}, u32[]{:S(2)}, u32[]{:S(2)}) collective-permute-start(bf16[32,4096]{1,0:T(8,128)(2,1)} %get-tuple-element.1028), channel_id=1, source_target_pairs={{0,32},{32,64},{64,96},{96,128},{128,160},{160,192},{192,224},{1,3... | collective-permute-start | bytes 786440 | tf_op jit(solution)/shard_map/while/body/eval_jaxpr/ppermute | solution.py:16
  738.9 26.0 %collective-permute-start.2 = (bf16[32,4096]{1,0:T(8,128)(2,1)}, bf16[32,4096]{1,0:T(8,128)(2,1)}, u32[]{:S(2)}, u32[]{:S(2)}) collective-permute-start(bf16[32,4096]{1,0:T(8,128)(2,1)} %fusion.332), channel_id=1, source_target_pairs={{32,0},{64,32},{96,64},{128,96},{160,128},{192,160},{224,192},{33,... | collective-permute-start | bytes 786440 | tf_op jit(solution)/shard_map/while/body/eval_jaxpr/ppermute | solution.py:16
  742.6 22.3 %collective-permute-start.3 = (bf16[32,4096]{1,0:T(8,128)(2,1)}, bf16[32,4096]{1,0:T(8,128)(2,1)}, u32[]{:S(2)}, u32[]{:S(2)}) collective-permute-start(bf16[32,4096]{1,0:T(8,128)(2,1)} %get-tuple-element.1028), channel_id=1, source_target_pairs={{0,32},{32,64},{64,96},{96,128},{128,160},{160,192},{192,224},{1,3... | collective-permute-start | bytes 786440 | tf_op jit(solution)/shard_map/while/body/eval_jaxpr/ppermute | solution.py:16
  764.9 26.0 %copy-start.7 = (f32[4096,128]{1,0:T(8,128)S(1)}, f32[4096,128]{1,0:T(8,128)}, u32[]{:S(2)}) copy-start(f32[4096,128]{1,0:T(8,128)} %get-tuple-element.610) | copy-start | bytes 6291460
  766.8 57.8 %copy-start.5 = (f32[128,4096]{1,0:T(8,128)S(1)}, f32[128,4096]{1,0:T(8,128)}, u32[]{:S(2)}) copy-start(f32[128,4096]{1,0:T(8,128)} %get-tuple-element.611) | copy-start | bytes 6291460
  766.8 24.1 %collective-permute-start.19 = (bf16[128,4096]{1,0:T(8,128)(2,1)S(1)}, bf16[128,4096]{1,0:T(8,128)(2,1)S(1)}, u32[]{:S(2)}, u32[]{:S(2)}) collective-permute-start(bf16[128,4096]{1,0:T(8,128)(2,1)S(1)} %convert_element_type.624), channel_id=1, source_target_pairs={{0,32},{32,0},{64,96},{96,64},{128,160},{160,128},{192,224},{224,1... | collective-permute-start | bytes 3145736 | tf_op jit(solution)/shard_map/ppermute | solution.py:10
  790.9 26.0 %collective-permute-start.20 = (bf16[128,4096]{1,0:T(8,128)(2,1)S(1)}, bf16[128,4096]{1,0:T(8,128)(2,1)S(1)}, u32[]{:S(2)}, u32[]{:S(2)}) collective-permute-start(bf16[128,4096]{1,0:T(8,128)(2,1)S(1)} %collective-permute-done.19), channel_id=1, source_target_pairs={{0,64},{32,96},{64,0},{96,32},{128,192},{160,224},{192,128},{224,1... | collective-permute-start | bytes 3145736 | tf_op jit(solution)/shard_map/ppermute | solution.py:10
  791.0 33.7 %collective-permute-start.16 = (bf16[4096,128]{1,0:T(8,128)(2,1)S(1)}, bf16[4096,128]{1,0:T(8,128)(2,1)}, u32[]{:S(2)}, u32[]{:S(2)}) collective-permute-start(bf16[4096,128]{1,0:T(8,128)(2,1)S(1)} %convert_element_type.619), channel_id=1, source_target_pairs={{0,32},{32,0},{64,96},{96,64},{128,160},{160,128},{192,224},{224,1... | collective-permute-start | bytes 3145736 | tf_op jit(solution)/shard_map/ppermute | solution.py:10
  816.9 27.6 %collective-permute-start.21 = (bf16[128,4096]{1,0:T(8,128)(2,1)S(1)}, bf16[128,4096]{1,0:T(8,128)(2,1)S(1)}, u32[]{:S(2)}, u32[]{:S(2)}) collective-permute-start(bf16[128,4096]{1,0:T(8,128)(2,1)S(1)} %collective-permute-done.20), channel_id=1, source_target_pairs={{0,128},{32,160},{64,192},{96,224},{128,0},{160,32},{192,64},{224,... | collective-permute-start | bytes 3145736 | tf_op jit(solution)/shard_map/ppermute | solution.py:10
  824.7 36.7 %collective-permute-start.17 = (bf16[4096,128]{1,0:T(8,128)(2,1)}, bf16[4096,128]{1,0:T(8,128)(2,1)}, u32[]{:S(2)}, u32[]{:S(2)}) collective-permute-start(bf16[4096,128]{1,0:T(8,128)(2,1)} %collective-permute-done.16), channel_id=1, source_target_pairs={{0,64},{32,96},{64,0},{96,32},{128,192},{160,224},{192,128},{224,1... | collective-permute-start | bytes 3145736 | tf_op jit(solution)/shard_map/ppermute | solution.py:10
  845.8 15.6 %copy-start.6 = (f32[4096,128]{1,0:T(8,128)S(1)}, f32[4096,128]{1,0:T(8,128)}, u32[]{:S(2)}) copy-start(f32[4096,128]{1,0:T(8,128)} %get-tuple-element.609) | copy-start | bytes 6291460
  848.2 236.5 %reduce-scatter.5.cloned.1.call-start = ((), (), s32[]{:S(2)}) async-start(), calls=%async_computation.4 | async-start | bytes 1081344 | tf_op jit(solution)/shard_map/reduce_scatter | solution.py:199
  861.4 16.6 %collective-permute-start.18 = (bf16[4096,128]{1,0:T(8,128)(2,1)}, bf16[4096,128]{1,0:T(8,128)(2,1)S(1)}, u32[]{:S(2)}, u32[]{:S(2)}) collective-permute-start(bf16[4096,128]{1,0:T(8,128)(2,1)} %collective-permute-done.17), channel_id=1, source_target_pairs={{0,128},{32,160},{64,192},{96,224},{128,0},{160,32},{192,64},{224,... | collective-permute-start | bytes 3145736 | tf_op jit(solution)/shard_map/ppermute | solution.py:10
  861.5 26.7 %copy-start.11 = (u32[256]{0:T(256)S(1)}, u32[256]{0:T(256)}, u32[]{:S(2)}) copy-start(u32[256]{0:T(256)} %constant.306) | copy-start | bytes 3076
  879.3 5.2 collective-permute-start.13
  884.6 3.7 collective-permute-start.14
  888.2 5.2 collective-permute-start.15
  (70 other events, 220.5 us)
Sparse Core Ops, SparseCore 0:
  24.0 67.8 all-gather.2
  94.4 62.8 all-gather.4
  848.3 119.7 reduce-scatter.6
  970.5 114.1 reduce-scatter.4
where the time goes:
time: 1100 us; the launch traced here: 1090 us
  waiting for transfers between devices  374 us (34%)
  matrix products  304 us (28%)
  starting transfers between devices  181 us (16%)
  other arithmetic  108 us (10%)
  blocking collectives  91.4 us (8%)
  local copies, waits for them, and re-layouts  15.7 us (1%)
  between operations  14.6 us (1%)
    ppermute x36, starting transfers between devices, passed_along(): lax.ppermute(value, axis, [(source, source + steps) for source in range(i...  138 us
    dot_general x54, matrix products, apply_layer(): jnp.dot(reduced, second_weight, preferred_element_type=jnp.float32)  122 us
    ppermute x18, waiting for transfers between devices, partner(): lax.ppermute(shard, axis, [(i, i ^ 1 << distance) for i in range(lax.axis...  120 us
    reduce_scatter x1, waiting for transfers between devices, per_device(): lax.psum_scatter(pair_sums[1].astype(jnp.bfloat16), 'dp', scatter_dimensi...  115 us
    dot_general x72, matrix products, apply_layer(): jnp.einsum('hqk,khd->qhd', probabilities, split_heads, preferred_element_...  77 us
    dot_general x36, matrix products, apply_layer(): jnp.dot(mixed_heads, first_weight, preferred_element_type=jnp.float32)  69.7 us
    all_gather x1, waiting for transfers between devices, per_device(): lax.all_gather(stacked[1], 'dp', axis=1, tiled=True)  65.1 us
    ppermute x36, waiting for transfers between devices, passed_along(): lax.ppermute(value, axis, [(source, source + steps) for source in range(i...  54.4 us
  transfers between devices with their start and end apart: 58, of which 29 were waited for; matrix products, arithmetic and copies ran while one was open for 20% of the time, Pallas kernels for 0%

commit v1 on v0

--- a/solution.py
+++ b/solution.py
@@ -107,7 +107,9 @@
     )
     full_gain, full_first, full_second = (
         lax.all_gather(stacked[0], "dp", axis=1, tiled=True),
-        lax.all_gather(stacked[1], "dp", axis=1, tiled=True),
+        jnp.concatenate(
+            lax.all_to_all(jnp.stack(lax.axis_size("dp") * [stacked[1]], 0), "dp", 0, 0), 1
+        ),
         lax.all_gather(stacked[2], "dp", axis=2, tiled=True),
     )
 

time: 1100 us -> 1060 us (0.964)
  waiting for transfers between devices: 374 us -> 304 us
  blocking collectives: 91.4 us -> 119 us
  local copies, waits for them, and re-layouts: 15.7 us -> 32.5 us
  other arithmetic: 108 us -> 94.3 us
    all_gather x1 -> x0, waiting for transfers between devices: 65.1 us -> none  [per_device(): lax.all_gather(stacked[1], 'dp', axis=1, tiled=True)]
    all_gather x1, blocking collectives: 37.2 us -> 64.8 us  [per_device(): lax.all_gather(stacked[0], 'dp', axis=1, tiled=True)]
  transfers between devices with their start and end apart: 58 -> 58, of which waited for: 29 -> 28; matrix products, arithmetic and copies ran while one was open for 20% -> 21% of each run, Pallas kernels for 0% -> 0%
where the time goes in v1:
time: 1060 us
  matrix products  306 us (29%)
  waiting for transfers between devices  304 us (29%)
  starting transfers between devices  185 us (17%)
  blocking collectives  119 us (11%)
  other arithmetic  94.3 us (9%)
  local copies, waits for them, and re-layouts  32.5 us (3%)
  between operations  14.6 us (1%)
    ppermute x36, starting transfers between devices, passed_along(): lax.ppermute(value, axis, [(source, source + steps) for source in range(i...  138 us
    dot_general x54, matrix products, apply_layer(): jnp.dot(reduced, second_weight, preferred_element_type=jnp.float32)  122 us
    reduce_scatter x1, waiting for transfers between devices, per_device(): lax.psum_scatter(pair_sums[1].astype(jnp.bfloat16), 'dp', scatter_dimensi...  115 us
    ppermute x18, waiting for transfers between devices, partner(): lax.ppermute(shard, axis, [(i, i ^ 1 << distance) for i in range(lax.axis...  112 us
    dot_general x72, matrix products, apply_layer(): jnp.einsum('hqk,khd->qhd', probabilities, split_heads, preferred_element_...  78.6 us
    dot_general x36, matrix products, apply_layer(): jnp.dot(mixed_heads, first_weight, preferred_element_type=jnp.float32)  69.8 us
    all_gather x1, blocking collectives, per_device(): lax.all_gather(stacked[0], 'dp', axis=1, tiled=True)  64.8 us
    ppermute x36, waiting for transfers between devices, passed_along(): lax.ppermute(value, axis, [(source, source + steps) for source in range(i...  54.9 us
  transfers between devices with their start and end apart: 58, of which 28 were waited for; matrix products, arithmetic and copies ran while one was open for 21% of the time, Pallas kernels for 0%

profile of v1, /device:TPU:2, one launch (start us, length us, event | category | flops | bytes accessed | tf_op | source)
XLA Modules:
  0.0 1059.6 jit_solution(1210736387638597345)
XLA Ops:
  25.5 9.5 all-to-all-start
  50.6 64.8 %all_gather.7 = bf16[2,4096]{1,0:T(2,128)(2,1)S(1)} all-gather(bf16[2,128]{1,0:T(2,128)(2,1)S(1)} %pad_maximum_fusion.2), channel_id=1, replica_groups=mesh['pipe'=8,'dp'=32] {'dp'}, dimensions={1}, use_global_device_ids=true | all-gather | bytes 16896 | tf_op jit(solution)/shard_map/all_gather | solution.py:109
  119.4 292.0 %while.49 = (s32[]{:T(128)}, bf16[32,4096]{1,0:T(8,128)(2,1)}, bf16[32,4096]{1,0:T(8,128)(2,1)}, bf16[2,2,32,4096]{3,2,1,0:T(8,128)(2,1)S(1)}, pred[]{:T(512)}, ...) while((s32[]{:T(128)}, bf16[32,4096]{1,0:T(8,128)(2,1)}, ...), condition=%wide.region_8.9_spmd, body=%wide.region_1.8_spmd.sunk | while | flops 172771520 | bytes 16375527 | solution.py:142
  131.4 5.1 collective-permute-start.1
  145.0 10.4 collective-permute-done
  176.4 5.4 collective-permute-start
  181.8 6.4 collective-permute-done
  209.1 5.4 collective-permute-start
  214.5 5.5 collective-permute-done
  240.9 5.4 collective-permute-start
  246.3 5.4 collective-permute-done
  272.7 5.4 collective-permute-start
  278.1 5.4 collective-permute-done
  304.5 5.4 collective-permute-start
  309.9 5.4 collective-permute-done
  336.2 5.4 collective-permute-start
  341.7 5.4 collective-permute-done
  368.0 5.4 collective-permute-start
  373.4 5.4 collective-permute-done
  399.8 5.4 collective-permute-start
  405.2 5.4 collective-permute-done
  412.8 318.1 %while.50 = (s32[]{:T(128)}, bf16[32,4096]{1,0:T(8,128)(2,1)}, bf16[32,4096]{1,0:T(8,128)(2,1)}, f32[4096]{0:T(1024)S(1)}, f32[4096,128]{1,0:T(8,128)}, /*index=...) while((s32[]{:T(128)}, bf16[32,4096]{1,0:T(8,128)(2,1)}, ...), condition=%wide.region_20.21_spmd.clone, body=%wide.region_9.20_spmd.clone.sunk | while | flops 456771968 | bytes 64646480 | solution.py:179
  424.5 5.4 collective-permute-start.3
  457.4 4.5 collective-permute-start.3
  465.1 3.8 fusion.335
  472.4 3.8 fusion.338
  489.6 3.7 collective-permute-start.2
  493.3 4.5 collective-permute-start.3
  500.9 3.8 fusion.335
  508.3 3.8 fusion.338
  525.4 3.7 collective-permute-start.2
  529.1 4.5 collective-permute-start.3
  536.8 3.8 fusion.335
  544.1 3.8 fusion.338
  561.3 3.7 collective-permute-start.2
  565.0 4.5 collective-permute-start.3
  572.7 3.8 fusion.335
  580.0 3.8 fusion.338
  597.2 3.7 collective-permute-start.2
  600.9 4.5 collective-permute-start.3
  608.6 3.8 fusion.335
  615.9 3.8 fusion.338
  633.0 3.7 collective-permute-start.2
  636.8 4.5 collective-permute-start.3
  644.4 3.8 fusion.335
  651.8 3.8 fusion.338
  672.6 4.5 collective-permute-start.3
  680.3 3.8 fusion.335
  687.6 3.8 fusion.338
  708.5 4.5 collective-permute-start.3
  716.2 3.8 fusion.335
  723.5 3.8 fusion.338
  732.7 4.7 collective-permute-start.19
  737.5 19.9 %collective-permute-done.19 = bf16[128,4096]{1,0:T(8,128)(2,1)S(1)} collective-permute-done((bf16[128,4096]{1,0:T(8,128)(2,1)S(1)}, bf16[128,4096]{1,0:T(8,128)(2,1)S(1)}, u32[]{:S(2)}, u32[]{:S(2)}) %collective-permute-start.19) | collective-permute-done | bytes 1048608 | tf_op jit(solution)/shard_map/ppermute | solution.py:10
  757.5 3.9 collective-permute-start.16
  761.4 22.0 %collective-permute-done.20 = bf16[128,4096]{1,0:T(8,128)(2,1)S(1)} collective-permute-done((bf16[128,4096]{1,0:T(8,128)(2,1)S(1)}, bf16[128,4096]{1,0:T(8,128)(2,1)S(1)}, u32[]{:S(2)}, u32[]{:S(2)}) %collective-permute-start.20) | collective-permute-done | bytes 1048608 | tf_op jit(solution)/shard_map/ppermute | solution.py:10
  783.4 7.6 collective-permute-start.21
  791.9 20.9 %collective-permute-done.21 = bf16[128,4096]{1,0:T(8,128)(2,1)S(1)} collective-permute-done((bf16[128,4096]{1,0:T(8,128)(2,1)S(1)}, bf16[128,4096]{1,0:T(8,128)(2,1)S(1)}, u32[]{:S(2)}, u32[]{:S(2)}) %collective-permute-start.21) | collective-permute-done | bytes 1048608 | tf_op jit(solution)/shard_map/ppermute | solution.py:10
  816.6 10.4 collective-permute-done.17
  827.1 16.5 %collective-permute-done.18 = bf16[4096,128]{1,0:T(8,128)(2,1)S(1)} collective-permute-done((bf16[4096,128]{1,0:T(8,128)(2,1)}, bf16[4096,128]{1,0:T(8,128)(2,1)S(1)}, u32[]{:S(2)}, u32[]{:S(2)}) %collective-permute-start.18) | collective-permute-done | bytes 1048608 | tf_op jit(solution)/shard_map/ppermute | solution.py:10
  855.1 3.9 collective-permute-done.15
  859.0 54.2 %all-reduce = bf16[4096]{0:T(1024)(128)(2,1)S(1)} all-reduce(bf16[4096]{0:T(1024)(128)(2,1)S(1)} %add_convert_fusion.2), channel_id=2, replica_groups=mesh['pipe'=8,'dp'=32] {'dp'}, use_global_device_ids=true, to_apply=%region_21.22.clone | all-reduce | flops 4096 | bytes 16384
  913.8 21.2 %reduce-scatter.7.cloned.1.call-done = bf16[128,128]{1,0:T(8,128)(2,1)} async-done(((bf16[4096,128]{1,0:T(8,128)(2,1)}), bf16[128,128]{1,0:T(8,128)(2,1)}) %reduce-scatter.7.cloned.1.call-update) | async-done | bytes 32784
  936.5 115.2 %reduce-scatter.5.cloned.1.call-done = bf16[128,128]{1,0:T(8,128)(2,1)} async-done(((bf16[4096,128]{1,0:T(8,128)(2,1)}), bf16[128,128]{1,0:T(8,128)(2,1)}) %reduce-scatter.5.cloned.1.call-update) | async-done | bytes 32784 | tf_op jit(solution)/shard_map/reduce_scatter | solution.py:201
  (760 shorter events, 442.3 us)
Async XLA Ops:
  7.2 5.7 collective-permute-start.7
  10.4 5.6 collective-permute-start.4
  12.9 4.6 collective-permute-start.8
  16.1 4.2 collective-permute-start.5
  17.5 5.4 collective-permute-start.9
  20.2 14.9 %collective-permute-start.6 = (bf16[1,128,128]{2,1,0:T(8,128)(2,1)S(1)}, bf16[1,128,128]{2,1,0:T(8,128)(2,1)S(1)}, u32[]{:S(2)}, u32[]{:S(2)}) collective-permute-start(bf16[1,128,128]{2,1,0:T(8,128)(2,1)S(1)} %collective-permute-done.5), channel_id=1, source_target_pairs={{0,128},{32,160},{64,192},{96,224},{128,0},{160,32},{192,64},{224,... | collective-permute-start | bytes 98312 | tf_op jit(solution)/shard_map/ppermute | solution.py:10
  25.5 13.4 %copy-start.13 = (s32[2,2]{1,0:T(2,128)S(1)}, s32[2,2]{1,0:T(2,128)}, u32[]{:S(2)}) copy-start(s32[2,2]{1,0:T(2,128)} %param.18) | copy-start | bytes 52
  25.5 13.5 %copy-start.12 = (s32[2,2,4]{2,1,0:T(2,128)S(1)}, s32[2,2,4]{2,1,0:T(2,128)}, u32[]{:S(2)}) copy-start(s32[2,2,4]{2,1,0:T(2,128)} %param.17) | copy-start | bytes 196
  25.5 89.9 %all-to-all-start = ((bf16[32,2,128,128]{3,2,1,0:T(8,128)(2,1)}), bf16[32,2,128,128]{3,2,1,0:T(8,128)(2,1)}, u32[]{:S(2)}, u32[]{:S(2)}) async-start(bf16[32,2,128,128]{3,2,1,0:T(8,128)(2,1)} %stack.2), calls=%async_computation | async-start | bytes 4194304 | tf_op jit(solution)/shard_map/all_to_all | solution.py:111
  35.1 82.8 %all-gather.2.cloned.1.call-start = ((), (), s32[]{:S(2)}) async-start(), calls=%async_computation.3 | async-start | bytes 2162688 | tf_op jit(solution)/shard_map/all_gather | solution.py:113
  35.8 899.2 %reduce-scatter.7.cloned.1.call-start = ((), (), s32[]{:S(2)}) async-start(), calls=%async_computation.5 | async-start | bytes 1081344
  35.9 6.1 collective-permute-start.10
  42.0 3.6 collective-permute-start.11
  45.5 5.1 collective-permute-start.12
  131.4 13.6 %collective-permute-start.1 = (bf16[32,4096]{1,0:T(8,128)(2,1)}, bf16[32,4096]{1,0:T(8,128)(2,1)}, u32[]{:S(2)}, u32[]{:S(2)}) collective-permute-start(bf16[32,4096]{1,0:T(8,128)(2,1)} %fusion.286), channel_id=1, source_target_pairs={{32,0},{64,32},{96,64},{128,96},{160,128},{192,160},{224,192},{33,... | collective-permute-start | bytes 786440 | tf_op jit(solution)/shard_map/while/body/eval_jaxpr/ppermute | solution.py:16
  142.8 12.7 %collective-permute-start = (bf16[32,4096]{1,0:T(8,128)(2,1)}, bf16[32,4096]{1,0:T(8,128)(2,1)S(1)}, u32[]{:S(2)}, u32[]{:S(2)}) collective-permute-start(bf16[32,4096]{1,0:T(8,128)(2,1)} %fusion.281), channel_id=1, source_target_pairs={{0,32},{32,64},{64,96},{96,128},{128,160},{160,192},{192,224},{1,3... | collective-permute-start | bytes 786440 | tf_op jit(solution)/shard_map/while/body/eval_jaxpr/ppermute | solution.py:16
  168.2 13.6 %collective-permute-start.1 = (bf16[32,4096]{1,0:T(8,128)(2,1)}, bf16[32,4096]{1,0:T(8,128)(2,1)}, u32[]{:S(2)}, u32[]{:S(2)}) collective-permute-start(bf16[32,4096]{1,0:T(8,128)(2,1)} %fusion.286), channel_id=1, source_target_pairs={{32,0},{64,32},{96,64},{128,96},{160,128},{192,160},{224,192},{33,... | collective-permute-start | bytes 786440 | tf_op jit(solution)/shard_map/while/body/eval_jaxpr/ppermute | solution.py:16
  176.4 11.8 %collective-permute-start = (bf16[32,4096]{1,0:T(8,128)(2,1)}, bf16[32,4096]{1,0:T(8,128)(2,1)S(1)}, u32[]{:S(2)}, u32[]{:S(2)}) collective-permute-start(bf16[32,4096]{1,0:T(8,128)(2,1)} %fusion.281), channel_id=1, source_target_pairs={{0,32},{32,64},{64,96},{96,128},{128,160},{160,192},{192,224},{1,3... | collective-permute-start | bytes 786440 | tf_op jit(solution)/shard_map/while/body/eval_jaxpr/ppermute | solution.py:16
  200.9 13.6 %collective-permute-start.1 = (bf16[32,4096]{1,0:T(8,128)(2,1)}, bf16[32,4096]{1,0:T(8,128)(2,1)}, u32[]{:S(2)}, u32[]{:S(2)}) collective-permute-start(bf16[32,4096]{1,0:T(8,128)(2,1)} %fusion.286), channel_id=1, source_target_pairs={{32,0},{64,32},{96,64},{128,96},{160,128},{192,160},{224,192},{33,... | collective-permute-start | bytes 786440 | tf_op jit(solution)/shard_map/while/body/eval_jaxpr/ppermute | solution.py:16
  209.1 10.9 %collective-permute-start = (bf16[32,4096]{1,0:T(8,128)(2,1)}, bf16[32,4096]{1,0:T(8,128)(2,1)S(1)}, u32[]{:S(2)}, u32[]{:S(2)}) collective-permute-start(bf16[32,4096]{1,0:T(8,128)(2,1)} %fusion.281), channel_id=1, source_target_pairs={{0,32},{32,64},{64,96},{96,128},{128,160},{160,192},{192,224},{1,3... | collective-permute-start | bytes 786440 | tf_op jit(solution)/shard_map/while/body/eval_jaxpr/ppermute | solution.py:16
  232.8 13.6 %collective-permute-start.1 = (bf16[32,4096]{1,0:T(8,128)(2,1)}, bf16[32,4096]{1,0:T(8,128)(2,1)}, u32[]{:S(2)}, u32[]{:S(2)}) collective-permute-start(bf16[32,4096]{1,0:T(8,128)(2,1)} %fusion.286), channel_id=1, source_target_pairs={{32,0},{64,32},{96,64},{128,96},{160,128},{192,160},{224,192},{33,... | collective-permute-start | bytes 786440 | tf_op jit(solution)/shard_map/while/body/eval_jaxpr/ppermute | solution.py:16
  240.9 10.9 %collective-permute-start = (bf16[32,4096]{1,0:T(8,128)(2,1)}, bf16[32,4096]{1,0:T(8,128)(2,1)S(1)}, u32[]{:S(2)}, u32[]{:S(2)}) collective-permute-start(bf16[32,4096]{1,0:T(8,128)(2,1)} %fusion.281), channel_id=1, source_target_pairs={{0,32},{32,64},{64,96},{96,128},{128,160},{160,192},{192,224},{1,3... | collective-permute-start | bytes 786440 | tf_op jit(solution)/shard_map/while/body/eval_jaxpr/ppermute | solution.py:16
  264.5 13.6 %collective-permute-start.1 = (bf16[32,4096]{1,0:T(8,128)(2,1)}, bf16[32,4096]{1,0:T(8,128)(2,1)}, u32[]{:S(2)}, u32[]{:S(2)}) collective-permute-start(bf16[32,4096]{1,0:T(8,128)(2,1)} %fusion.286), channel_id=1, source_target_pairs={{32,0},{64,32},{96,64},{128,96},{160,128},{192,160},{224,192},{33,... | collective-permute-start | bytes 786440 | tf_op jit(solution)/shard_map/while/body/eval_jaxpr/ppermute | solution.py:16
  272.7 10.9 %collective-permute-start = (bf16[32,4096]{1,0:T(8,128)(2,1)}, bf16[32,4096]{1,0:T(8,128)(2,1)S(1)}, u32[]{:S(2)}, u32[]{:S(2)}) collective-permute-start(bf16[32,4096]{1,0:T(8,128)(2,1)} %fusion.281), channel_id=1, source_target_pairs={{0,32},{32,64},{64,96},{96,128},{128,160},{160,192},{192,224},{1,3... | collective-permute-start | bytes 786440 | tf_op jit(solution)/shard_map/while/body/eval_jaxpr/ppermute | solution.py:16
  296.3 13.6 %collective-permute-start.1 = (bf16[32,4096]{1,0:T(8,128)(2,1)}, bf16[32,4096]{1,0:T(8,128)(2,1)}, u32[]{:S(2)}, u32[]{:S(2)}) collective-permute-start(bf16[32,4096]{1,0:T(8,128)(2,1)} %fusion.286), channel_id=1, source_target_pairs={{32,0},{64,32},{96,64},{128,96},{160,128},{192,160},{224,192},{33,... | collective-permute-start | bytes 786440 | tf_op jit(solution)/shard_map/while/body/eval_jaxpr/ppermute | solution.py:16
  304.5 10.9 %collective-permute-start = (bf16[32,4096]{1,0:T(8,128)(2,1)}, bf16[32,4096]{1,0:T(8,128)(2,1)S(1)}, u32[]{:S(2)}, u32[]{:S(2)}) collective-permute-start(bf16[32,4096]{1,0:T(8,128)(2,1)} %fusion.281), channel_id=1, source_target_pairs={{0,32},{32,64},{64,96},{96,128},{128,160},{160,192},{192,224},{1,3... | collective-permute-start | bytes 786440 | tf_op jit(solution)/shard_map/while/body/eval_jaxpr/ppermute | solution.py:16
  328.1 13.6 %collective-permute-start.1 = (bf16[32,4096]{1,0:T(8,128)(2,1)}, bf16[32,4096]{1,0:T(8,128)(2,1)}, u32[]{:S(2)}, u32[]{:S(2)}) collective-permute-start(bf16[32,4096]{1,0:T(8,128)(2,1)} %fusion.286), channel_id=1, source_target_pairs={{32,0},{64,32},{96,64},{128,96},{160,128},{192,160},{224,192},{33,... | collective-permute-start | bytes 786440 | tf_op jit(solution)/shard_map/while/body/eval_jaxpr/ppermute | solution.py:16
  336.2 10.9 %collective-permute-start = (bf16[32,4096]{1,0:T(8,128)(2,1)}, bf16[32,4096]{1,0:T(8,128)(2,1)S(1)}, u32[]{:S(2)}, u32[]{:S(2)}) collective-permute-start(bf16[32,4096]{1,0:T(8,128)(2,1)} %fusion.281), channel_id=1, source_target_pairs={{0,32},{32,64},{64,96},{96,128},{128,160},{160,192},{192,224},{1,3... | collective-permute-start | bytes 786440 | tf_op jit(solution)/shard_map/while/body/eval_jaxpr/ppermute | solution.py:16
  359.9 13.6 %collective-permute-start.1 = (bf16[32,4096]{1,0:T(8,128)(2,1)}, bf16[32,4096]{1,0:T(8,128)(2,1)}, u32[]{:S(2)}, u32[]{:S(2)}) collective-permute-start(bf16[32,4096]{1,0:T(8,128)(2,1)} %fusion.286), channel_id=1, source_target_pairs={{32,0},{64,32},{96,64},{128,96},{160,128},{192,160},{224,192},{33,... | collective-permute-start | bytes 786440 | tf_op jit(solution)/shard_map/while/body/eval_jaxpr/ppermute | solution.py:16
  368.0 10.9 %collective-permute-start = (bf16[32,4096]{1,0:T(8,128)(2,1)}, bf16[32,4096]{1,0:T(8,128)(2,1)S(1)}, u32[]{:S(2)}, u32[]{:S(2)}) collective-permute-start(bf16[32,4096]{1,0:T(8,128)(2,1)} %fusion.281), channel_id=1, source_target_pairs={{0,32},{32,64},{64,96},{96,128},{128,160},{160,192},{192,224},{1,3... | collective-permute-start | bytes 786440 | tf_op jit(solution)/shard_map/while/body/eval_jaxpr/ppermute | solution.py:16
  391.7 13.6 %collective-permute-start.1 = (bf16[32,4096]{1,0:T(8,128)(2,1)}, bf16[32,4096]{1,0:T(8,128)(2,1)}, u32[]{:S(2)}, u32[]{:S(2)}) collective-permute-start(bf16[32,4096]{1,0:T(8,128)(2,1)} %fusion.286), channel_id=1, source_target_pairs={{32,0},{64,32},{96,64},{128,96},{160,128},{192,160},{224,192},{33,... | collective-permute-start | bytes 786440 | tf_op jit(solution)/shard_map/while/body/eval_jaxpr/ppermute | solution.py:16
  399.8 10.9 %collective-permute-start = (bf16[32,4096]{1,0:T(8,128)(2,1)}, bf16[32,4096]{1,0:T(8,128)(2,1)S(1)}, u32[]{:S(2)}, u32[]{:S(2)}) collective-permute-start(bf16[32,4096]{1,0:T(8,128)(2,1)} %fusion.281), channel_id=1, source_target_pairs={{0,32},{32,64},{64,96},{96,128},{128,160},{160,192},{192,224},{1,3... | collective-permute-start | bytes 786440 | tf_op jit(solution)/shard_map/while/body/eval_jaxpr/ppermute | solution.py:16
  422.6 22.2 %collective-permute-start.2 = (bf16[32,4096]{1,0:T(8,128)(2,1)}, bf16[32,4096]{1,0:T(8,128)(2,1)}, u32[]{:S(2)}, u32[]{:S(2)}) collective-permute-start(bf16[32,4096]{1,0:T(8,128)(2,1)} %fusion.332), channel_id=1, source_target_pairs={{32,0},{64,32},{96,64},{128,96},{160,128},{192,160},{224,192},{33,... | collective-permute-start | bytes 786440 | tf_op jit(solution)/shard_map/while/body/eval_jaxpr/ppermute | solution.py:16
  424.5 20.3 %collective-permute-start.3 = (bf16[32,4096]{1,0:T(8,128)(2,1)}, bf16[32,4096]{1,0:T(8,128)(2,1)}, u32[]{:S(2)}, u32[]{:S(2)}) collective-permute-start(bf16[32,4096]{1,0:T(8,128)(2,1)} %get-tuple-element.1028), channel_id=1, source_target_pairs={{0,32},{32,64},{64,96},{96,128},{128,160},{160,192},{192,224},{1,3... | collective-permute-start | bytes 786440 | tf_op jit(solution)/shard_map/while/body/eval_jaxpr/ppermute | solution.py:16
  454.6 25.1 %collective-permute-start.2 = (bf16[32,4096]{1,0:T(8,128)(2,1)}, bf16[32,4096]{1,0:T(8,128)(2,1)}, u32[]{:S(2)}, u32[]{:S(2)}) collective-permute-start(bf16[32,4096]{1,0:T(8,128)(2,1)} %fusion.332), channel_id=1, source_target_pairs={{32,0},{64,32},{96,64},{128,96},{160,128},{192,160},{224,192},{33,... | collective-permute-start | bytes 786440 | tf_op jit(solution)/shard_map/while/body/eval_jaxpr/ppermute | solution.py:16
  457.4 22.3 %collective-permute-start.3 = (bf16[32,4096]{1,0:T(8,128)(2,1)}, bf16[32,4096]{1,0:T(8,128)(2,1)}, u32[]{:S(2)}, u32[]{:S(2)}) collective-permute-start(bf16[32,4096]{1,0:T(8,128)(2,1)} %get-tuple-element.1028), channel_id=1, source_target_pairs={{0,32},{32,64},{64,96},{96,128},{128,160},{160,192},{192,224},{1,3... | collective-permute-start | bytes 786440 | tf_op jit(solution)/shard_map/while/body/eval_jaxpr/ppermute | solution.py:16
  489.6 26.0 %collective-permute-start.2 = (bf16[32,4096]{1,0:T(8,128)(2,1)}, bf16[32,4096]{1,0:T(8,128)(2,1)}, u32[]{:S(2)}, u32[]{:S(2)}) collective-permute-start(bf16[32,4096]{1,0:T(8,128)(2,1)} %fusion.332), channel_id=1, source_target_pairs={{32,0},{64,32},{96,64},{128,96},{160,128},{192,160},{224,192},{33,... | collective-permute-start | bytes 786440 | tf_op jit(solution)/shard_map/while/body/eval_jaxpr/ppermute | solution.py:16
  493.3 22.3 %collective-permute-start.3 = (bf16[32,4096]{1,0:T(8,128)(2,1)}, bf16[32,4096]{1,0:T(8,128)(2,1)}, u32[]{:S(2)}, u32[]{:S(2)}) collective-permute-start(bf16[32,4096]{1,0:T(8,128)(2,1)} %get-tuple-element.1028), channel_id=1, source_target_pairs={{0,32},{32,64},{64,96},{96,128},{128,160},{160,192},{192,224},{1,3... | collective-permute-start | bytes 786440 | tf_op jit(solution)/shard_map/while/body/eval_jaxpr/ppermute | solution.py:16
  525.4 26.0 %collective-permute-start.2 = (bf16[32,4096]{1,0:T(8,128)(2,1)}, bf16[32,4096]{1,0:T(8,128)(2,1)}, u32[]{:S(2)}, u32[]{:S(2)}) collective-permute-start(bf16[32,4096]{1,0:T(8,128)(2,1)} %fusion.332), channel_id=1, source_target_pairs={{32,0},{64,32},{96,64},{128,96},{160,128},{192,160},{224,192},{33,... | collective-permute-start | bytes 786440 | tf_op jit(solution)/shard_map/while/body/eval_jaxpr/ppermute | solution.py:16
  529.1 22.3 %collective-permute-start.3 = (bf16[32,4096]{1,0:T(8,128)(2,1)}, bf16[32,4096]{1,0:T(8,128)(2,1)}, u32[]{:S(2)}, u32[]{:S(2)}) collective-permute-start(bf16[32,4096]{1,0:T(8,128)(2,1)} %get-tuple-element.1028), channel_id=1, source_target_pairs={{0,32},{32,64},{64,96},{96,128},{128,160},{160,192},{192,224},{1,3... | collective-permute-start | bytes 786440 | tf_op jit(solution)/shard_map/while/body/eval_jaxpr/ppermute | solution.py:16
  561.3 26.0 %collective-permute-start.2 = (bf16[32,4096]{1,0:T(8,128)(2,1)}, bf16[32,4096]{1,0:T(8,128)(2,1)}, u32[]{:S(2)}, u32[]{:S(2)}) collective-permute-start(bf16[32,4096]{1,0:T(8,128)(2,1)} %fusion.332), channel_id=1, source_target_pairs={{32,0},{64,32},{96,64},{128,96},{160,128},{192,160},{224,192},{33,... | collective-permute-start | bytes 786440 | tf_op jit(solution)/shard_map/while/body/eval_jaxpr/ppermute | solution.py:16
  565.0 22.3 %collective-permute-start.3 = (bf16[32,4096]{1,0:T(8,128)(2,1)}, bf16[32,4096]{1,0:T(8,128)(2,1)}, u32[]{:S(2)}, u32[]{:S(2)}) collective-permute-start(bf16[32,4096]{1,0:T(8,128)(2,1)} %get-tuple-element.1028), channel_id=1, source_target_pairs={{0,32},{32,64},{64,96},{96,128},{128,160},{160,192},{192,224},{1,3... | collective-permute-start | bytes 786440 | tf_op jit(solution)/shard_map/while/body/eval_jaxpr/ppermute | solution.py:16
  597.2 26.0 %collective-permute-start.2 = (bf16[32,4096]{1,0:T(8,128)(2,1)}, bf16[32,4096]{1,0:T(8,128)(2,1)}, u32[]{:S(2)}, u32[]{:S(2)}) collective-permute-start(bf16[32,4096]{1,0:T(8,128)(2,1)} %fusion.332), channel_id=1, source_target_pairs={{32,0},{64,32},{96,64},{128,96},{160,128},{192,160},{224,192},{33,... | collective-permute-start | bytes 786440 | tf_op jit(solution)/shard_map/while/body/eval_jaxpr/ppermute | solution.py:16
  600.9 22.3 %collective-permute-start.3 = (bf16[32,4096]{1,0:T(8,128)(2,1)}, bf16[32,4096]{1,0:T(8,128)(2,1)}, u32[]{:S(2)}, u32[]{:S(2)}) collective-permute-start(bf16[32,4096]{1,0:T(8,128)(2,1)} %get-tuple-element.1028), channel_id=1, source_target_pairs={{0,32},{32,64},{64,96},{96,128},{128,160},{160,192},{192,224},{1,3... | collective-permute-start | bytes 786440 | tf_op jit(solution)/shard_map/while/body/eval_jaxpr/ppermute | solution.py:16
  633.0 26.0 %collective-permute-start.2 = (bf16[32,4096]{1,0:T(8,128)(2,1)}, bf16[32,4096]{1,0:T(8,128)(2,1)}, u32[]{:S(2)}, u32[]{:S(2)}) collective-permute-start(bf16[32,4096]{1,0:T(8,128)(2,1)} %fusion.332), channel_id=1, source_target_pairs={{32,0},{64,32},{96,64},{128,96},{160,128},{192,160},{224,192},{33,... | collective-permute-start | bytes 786440 | tf_op jit(solution)/shard_map/while/body/eval_jaxpr/ppermute | solution.py:16
  636.8 22.3 %collective-permute-start.3 = (bf16[32,4096]{1,0:T(8,128)(2,1)}, bf16[32,4096]{1,0:T(8,128)(2,1)}, u32[]{:S(2)}, u32[]{:S(2)}) collective-permute-start(bf16[32,4096]{1,0:T(8,128)(2,1)} %get-tuple-element.1028), channel_id=1, source_target_pairs={{0,32},{32,64},{64,96},{96,128},{128,160},{160,192},{192,224},{1,3... | collective-permute-start | bytes 786440 | tf_op jit(solution)/shard_map/while/body/eval_jaxpr/ppermute | solution.py:16
  668.9 26.0 %collective-permute-start.2 = (bf16[32,4096]{1,0:T(8,128)(2,1)}, bf16[32,4096]{1,0:T(8,128)(2,1)}, u32[]{:S(2)}, u32[]{:S(2)}) collective-permute-start(bf16[32,4096]{1,0:T(8,128)(2,1)} %fusion.332), channel_id=1, source_target_pairs={{32,0},{64,32},{96,64},{128,96},{160,128},{192,160},{224,192},{33,... | collective-permute-start | bytes 786440 | tf_op jit(solution)/shard_map/while/body/eval_jaxpr/ppermute | solution.py:16
  672.6 22.3 %collective-permute-start.3 = (bf16[32,4096]{1,0:T(8,128)(2,1)}, bf16[32,4096]{1,0:T(8,128)(2,1)}, u32[]{:S(2)}, u32[]{:S(2)}) collective-permute-start(bf16[32,4096]{1,0:T(8,128)(2,1)} %get-tuple-element.1028), channel_id=1, source_target_pairs={{0,32},{32,64},{64,96},{96,128},{128,160},{160,192},{192,224},{1,3... | collective-permute-start | bytes 786440 | tf_op jit(solution)/shard_map/while/body/eval_jaxpr/ppermute | solution.py:16
  704.8 26.0 %collective-permute-start.2 = (bf16[32,4096]{1,0:T(8,128)(2,1)}, bf16[32,4096]{1,0:T(8,128)(2,1)}, u32[]{:S(2)}, u32[]{:S(2)}) collective-permute-start(bf16[32,4096]{1,0:T(8,128)(2,1)} %fusion.332), channel_id=1, source_target_pairs={{32,0},{64,32},{96,64},{128,96},{160,128},{192,160},{224,192},{33,... | collective-permute-start | bytes 786440 | tf_op jit(solution)/shard_map/while/body/eval_jaxpr/ppermute | solution.py:16
  708.5 22.3 %collective-permute-start.3 = (bf16[32,4096]{1,0:T(8,128)(2,1)}, bf16[32,4096]{1,0:T(8,128)(2,1)}, u32[]{:S(2)}, u32[]{:S(2)}) collective-permute-start(bf16[32,4096]{1,0:T(8,128)(2,1)} %get-tuple-element.1028), channel_id=1, source_target_pairs={{0,32},{32,64},{64,96},{96,128},{128,160},{160,192},{192,224},{1,3... | collective-permute-start | bytes 786440 | tf_op jit(solution)/shard_map/while/body/eval_jaxpr/ppermute | solution.py:16
  730.9 26.5 %copy-start.5 = (f32[4096,128]{1,0:T(8,128)S(1)}, f32[4096,128]{1,0:T(8,128)}, u32[]{:S(2)}) copy-start(f32[4096,128]{1,0:T(8,128)} %get-tuple-element.610) | copy-start | bytes 6291460
  732.7 58.3 %copy-start.3 = (f32[128,4096]{1,0:T(8,128)S(1)}, f32[128,4096]{1,0:T(8,128)}, u32[]{:S(2)}) copy-start(f32[128,4096]{1,0:T(8,128)} %get-tuple-element.611) | copy-start | bytes 6291460
  732.7 24.6 %collective-permute-start.19 = (bf16[128,4096]{1,0:T(8,128)(2,1)S(1)}, bf16[128,4096]{1,0:T(8,128)(2,1)S(1)}, u32[]{:S(2)}, u32[]{:S(2)}) collective-permute-start(bf16[128,4096]{1,0:T(8,128)(2,1)S(1)} %convert_element_type.624), channel_id=1, source_target_pairs={{0,32},{32,0},{64,96},{96,64},{128,160},{160,128},{192,224},{224,1... | collective-permute-start | bytes 3145736 | tf_op jit(solution)/shard_map/ppermute | solution.py:10
  757.4 26.0 %collective-permute-start.20 = (bf16[128,4096]{1,0:T(8,128)(2,1)S(1)}, bf16[128,4096]{1,0:T(8,128)(2,1)S(1)}, u32[]{:S(2)}, u32[]{:S(2)}) collective-permute-start(bf16[128,4096]{1,0:T(8,128)(2,1)S(1)} %collective-permute-done.19), channel_id=1, source_target_pairs={{0,64},{32,96},{64,0},{96,32},{128,192},{160,224},{192,128},{224,1... | collective-permute-start | bytes 3145736 | tf_op jit(solution)/shard_map/ppermute | solution.py:10
  757.5 33.7 %collective-permute-start.16 = (bf16[4096,128]{1,0:T(8,128)(2,1)S(1)}, bf16[4096,128]{1,0:T(8,128)(2,1)}, u32[]{:S(2)}, u32[]{:S(2)}) collective-permute-start(bf16[4096,128]{1,0:T(8,128)(2,1)S(1)} %convert_element_type.619), channel_id=1, source_target_pairs={{0,32},{32,0},{64,96},{96,64},{128,160},{160,128},{192,224},{224,1... | collective-permute-start | bytes 3145736 | tf_op jit(solution)/shard_map/ppermute | solution.py:10
  783.4 29.4 %collective-permute-start.21 = (bf16[128,4096]{1,0:T(8,128)(2,1)S(1)}, bf16[128,4096]{1,0:T(8,128)(2,1)S(1)}, u32[]{:S(2)}, u32[]{:S(2)}) collective-permute-start(bf16[128,4096]{1,0:T(8,128)(2,1)S(1)} %collective-permute-done.20), channel_id=1, source_target_pairs={{0,128},{32,160},{64,192},{96,224},{128,0},{160,32},{192,64},{224,... | collective-permute-start | bytes 3145736 | tf_op jit(solution)/shard_map/ppermute | solution.py:10
  791.2 35.8 %collective-permute-start.17 = (bf16[4096,128]{1,0:T(8,128)(2,1)}, bf16[4096,128]{1,0:T(8,128)(2,1)}, u32[]{:S(2)}, u32[]{:S(2)}) collective-permute-start(bf16[4096,128]{1,0:T(8,128)(2,1)} %collective-permute-done.16), channel_id=1, source_target_pairs={{0,64},{32,96},{64,0},{96,32},{128,192},{160,224},{192,128},{224,1... | collective-permute-start | bytes 3145736 | tf_op jit(solution)/shard_map/ppermute | solution.py:10
  814.1 12.9 %copy-start.4 = (f32[4096,128]{1,0:T(8,128)S(1)}, f32[4096,128]{1,0:T(8,128)}, u32[]{:S(2)}) copy-start(f32[4096,128]{1,0:T(8,128)} %get-tuple-element.609) | copy-start | bytes 6291460
  816.5 235.1 %reduce-scatter.5.cloned.1.call-start = ((), (), s32[]{:S(2)}) async-start(), calls=%async_computation.4 | async-start | bytes 1081344 | tf_op jit(solution)/shard_map/reduce_scatter | solution.py:201
  827.0 16.6 %collective-permute-start.18 = (bf16[4096,128]{1,0:T(8,128)(2,1)}, bf16[4096,128]{1,0:T(8,128)(2,1)S(1)}, u32[]{:S(2)}, u32[]{:S(2)}) collective-permute-start(bf16[4096,128]{1,0:T(8,128)(2,1)} %collective-permute-done.17), channel_id=1, source_target_pairs={{0,128},{32,160},{64,192},{96,224},{128,0},{160,32},{192,64},{224,... | collective-permute-start | bytes 3145736 | tf_op jit(solution)/shard_map/ppermute | solution.py:10
  827.1 26.7 %copy-start.15 = (u32[256]{0:T(256)S(1)}, u32[256]{0:T(256)}, u32[]{:S(2)}) copy-start(u32[256]{0:T(256)} %constant.306) | copy-start | bytes 3076
  844.9 5.2 collective-permute-start.13
  850.2 3.7 collective-permute-start.14
  853.8 5.2 collective-permute-start.15
  (66 other events, 184.6 us)
Sparse Core Ops, SparseCore 0:
  38.2 79.5 all-gather.1
  816.6 118.2 reduce-scatter.6
  937.5 114.1 reduce-scatter.4
